TPU v7x, 512 devices: a whole 4x8x8 slice. The times are simulated.
512 devices in a mesh: dp: 32 (over z, x), param: 16 (over y, core).
Axes of the slice: x: 4, y: 8, z: 8, core: 2. Of those that a mesh axis runs over, the one named last changes fastest.
Arguments:
- features: bfloat16 [32768, 2048], P('dp'), may hold values from -24 to 24
- w_hidden: bfloat16 [2048, 2048], P(None, 'param'), may hold values from -0.125 to 0.125
- w_head: bfloat16 [2048, 36], P('param'), may hold values from -0.03125 to 0.03125
- base_mean: float32 [32768, 36], P('dp'), may hold values from -5 to 5
- actions: float32 [32768, 36], P('dp'), may hold values from -7 to 7
- advantages: float32 [32768], P('dp'), may hold values from -4 to 4
- log_std: float32 [36], replicated, may hold values from -1 to 0
Outputs:
- step_unit: float32 [2048, 2048], P('dp', 'param')
- kl_ratio: float32 [], replicated
All inputs are finite; a program needn't handle non-finite values.
Results may differ from a plain program's by a relative error of at most 0.0049.
Values may be sent and summed in bfloat16 or wider, within the bound.
A program may use at most 64 MiB of HBM per device.

v0:
```python
import jax
import jax.numpy as jnp
from jax import lax
from jax.sharding import PartitionSpec as P

D = 2048
UNITS = 2048
ITERS = 2
DAMPING = 0.01
TRIAL_KL = 4.0


def shards(features, w_hidden, w_head, base_mean, actions, advantages, log_std):
    highest = lax.Precision.HIGHEST
    rows = features.shape[0]
    width = features.shape[1]
    dp_count = lax.axis_size("dp")
    batch = rows * dp_count
    inv_var = jnp.exp(-2.0 * log_std)
    pre = jnp.dot(features, w_hidden, preferred_element_type=jnp.float32)
    hidden = jnp.tanh(pre)
    slope = 1.0 - hidden * hidden

    def head_total(part):
        return lax.psum(jnp.dot(part, w_head, preferred_element_type=jnp.float32), "param")

    mean = base_mean + head_total(hidden.astype(jnp.bfloat16))
    delta = advantages[:, None] * (actions - mean) * inv_var
    head_t = w_head.astype(jnp.float32).T

    def pull(moment):
        return (jnp.dot(moment, head_t, precision=highest) * slope / batch).astype(jnp.bfloat16)

    def rowsum(grads):
        term = lax.dot_general(
            features, grads, (((0,), (0,)), ((), ())), preferred_element_type=jnp.float32
        )
        return lax.psum(term, "dp")

    def expand(vector_b):
        return jnp.dot(features, vector_b, preferred_element_type=jnp.float32)

    def total(values):
        return lax.psum((values[0],), "param")

    grad = rowsum(pull(delta))
    solution = jnp.zeros_like(grad)
    resid = grad
    direction = grad
    (norm_now,) = total((jnp.sum(resid * resid),))
    for turn in range(ITERS):
        change = expand(direction.astype(jnp.bfloat16))
        dmu = head_total((change * slope).astype(jnp.bfloat16))
        image = rowsum(pull(dmu * inv_var)) + DAMPING * direction
        image, dmu = (image, dmu)
        (curv,) = total((jnp.sum(direction * image),))
        alpha = norm_now / curv
        solution = solution + alpha * direction
        resid = resid - alpha * image
        (norm_next,) = total((jnp.sum(resid * resid),))
        direction = resid + norm_next / norm_now * direction
        norm_now = norm_next
    (shs,) = total((jnp.sum(solution * (grad - resid)),))
    block = width // dp_count
    step_unit = lax.dynamic_slice_in_dim(
        solution * jnp.sqrt(D * UNITS / shs), lax.axis_index("dp") * block, block, 0
    )
    reach = jnp.sqrt(2.0 * TRIAL_KL / shs)
    moved = expand((reach * solution).astype(jnp.bfloat16))
    shift = (jnp.tanh(pre + moved) - hidden).astype(jnp.bfloat16)
    dmean = head_total(shift)
    kl_value = lax.psum(jnp.sum(dmean * dmean * inv_var) / (2.0 * batch), "dp")
    return (step_unit, kl_value / TRIAL_KL)


def solution(mesh):
    return jax.shard_map(
        shards,
        mesh=mesh,
        in_specs=(
            P("dp", None),
            P(None, "param"),
            P("param", None),
            P("dp", None),
            P("dp", None),
            P("dp"),
            P(),
        ),
        out_specs=(P("dp", "param"), P()),
        check_vma=False,
    )
```

profile of v0, /device:TPU:8, one launch (start us, length us, event | category | flops | bytes accessed | tf_op | source)
XLA Modules:
  0.0 1150.3 jit_solution(4026722061031804049)
XLA Ops:
  7.2 0.0 copy-start
  7.2 0.0 copy-start.3
  7.2 0.0 copy-start.7
  7.2 0.0 copy-start.5
  7.2 0.0 copy-start.4
  7.2 0.0 copy-start.6
  7.2 0.0 all-reduce.9.cloned.1.call-start
  7.3 0.9 copy-done
  8.2 3.4 fusion.42
  11.6 0.0 copy-done.3
  11.7 0.9 fusion.27
  12.6 0.0 all-reduce.9.cloned.1.call-update
  12.6 0.0 all-reduce.11.cloned.1.call-start
  12.7 0.0 copy-done.7
  12.7 112.3 %all-reduce.9.cloned.1.call-done = f32[1024,36]{0,1:T(8,128)} async-done(((f32[1024,36]{0,1:T(8,128)}), f32[1024,36]{0,1:T(8,128)}) %all-reduce.9.cloned.1.call-update) | async-done | bytes 147472 | tf_op jit(solution)/shard_map/psum | solution.py:25
  125.0 0.0 copy-done.5
  125.0 0.0 copy-done.4
  125.0 0.0 copy-done.6
  125.0 1.6 fusion.11
  126.6 4.0 convolution_bitcast_fusion.2
  130.5 0.0 all-reduce.11.cloned.1.call-update
  130.6 0.0 all-reduce.13.cloned.1.call-start
  130.6 160.6 %all-reduce.11.cloned.1.call-done = f32[2048,128]{0,1:T(8,128)} async-done(((f32[2048,128]{0,1:T(8,128)}), f32[2048,128]{0,1:T(8,128)}) %all-reduce.11.cloned.1.call-update) | async-done | bytes 1048592 | tf_op jit(solution)/shard_map/psum | solution.py:38
  291.2 4.7 fusion.16
  295.9 0.0 copy-start.1
  295.9 0.0 all-reduce.13.cloned.1.call-update
  295.9 0.0 all-reduce.15.cloned.1.call-start
  296.0 104.9 %all-reduce.13.cloned.1.call-done = f32[1024,36]{0,1:T(8,128)} async-done(((f32[1024,36]{0,1:T(8,128)}), f32[1024,36]{0,1:T(8,128)}) %all-reduce.13.cloned.1.call-update) | async-done | bytes 147472 | tf_op jit(solution)/shard_map/psum | solution.py:25
  400.8 1.6 fusion.10
  402.4 3.9 convolution_bitcast_fusion.1
  406.4 0.0 all-reduce.15.cloned.1.call-update
  406.4 0.0 all-reduce.17.cloned.1.call-start
  406.4 160.6 %all-reduce.15.cloned.1.call-done = f32[2048,128]{0,1:T(8,128)} async-done(((f32[2048,128]{0,1:T(8,128)}), f32[2048,128]{0,1:T(8,128)}) %all-reduce.15.cloned.1.call-update) | async-done | bytes 1048592 | tf_op jit(solution)/shard_map/psum | solution.py:38
  567.0 0.0 copy-done.1
  567.0 0.0 copy-start.2
  567.0 2.2 multiply_reduce_fusion.3
  569.2 21.2 %all-reduce = (f32[]{:T(128)}, f32[]{:T(128)}) all-reduce(f32[]{:T(128)} %get-tuple-element.5, f32[]{:T(128)} %get-tuple-element.4), channel_id=1, replica_groups=mesh['dp'=32,'param'=16] {'param'}, use_global_device_ids=true, to_apply=%region_3.0 | all-reduce | flops 2 | bytes 16 | tf_op jit(solution)/shard_map/psum | solution.py:44
  591.8 2.1 multiply_reduce_fusion.2
  593.9 24.2 %psum.97 = f32[]{:T(128)} all-reduce(f32[]{:T(128)} %multiply_reduce_fusion.2), channel_id=1, replica_groups=mesh['dp'=32,'param'=16] {'param'}, use_global_device_ids=true, to_apply=%region_9.0 | all-reduce | flops 1 | bytes 8 | tf_op jit(solution)/shard_map/psum | solution.py:44
  619.4 0.0 copy-done.2
  619.4 4.4 fusion.15
  623.7 0.0 all-reduce.17.cloned.1.call-update
  623.8 0.0 all-reduce.19.cloned.1.call-start
  623.8 107.6 %all-reduce.17.cloned.1.call-done = f32[1024,36]{0,1:T(8,128)} async-done(((f32[1024,36]{0,1:T(8,128)}), f32[1024,36]{0,1:T(8,128)}) %all-reduce.17.cloned.1.call-update) | async-done | bytes 147472 | tf_op jit(solution)/shard_map/psum | solution.py:25
  731.4 1.6 fusion.9
  733.0 3.9 convolution_bitcast_fusion
  737.0 0.0 all-reduce.19.cloned.1.call-update
  737.0 0.0 all-reduce.21.cloned.1.call-start
  737.0 160.6 %all-reduce.19.cloned.1.call-done = f32[2048,128]{0,1:T(8,128)} async-done(((f32[2048,128]{0,1:T(8,128)}), f32[2048,128]{0,1:T(8,128)}) %all-reduce.19.cloned.1.call-update) | async-done | bytes 1048592 | tf_op jit(solution)/shard_map/psum | solution.py:38
  897.6 2.2 multiply_reduce_fusion.1
  899.8 21.2 %psum.100 = f32[]{:T(128)} all-reduce(f32[]{:T(128)} %multiply_reduce_fusion.1), channel_id=1, replica_groups=mesh['dp'=32,'param'=16] {'param'}, use_global_device_ids=true, to_apply=%region_13.0 | all-reduce | flops 1 | bytes 8 | tf_op jit(solution)/shard_map/psum | solution.py:44
  922.4 3.4 multiply_reduce_fusion
  925.7 24.2 %psum.101 = f32[]{:T(128)} all-reduce(f32[]{:T(128)} %get-tuple-element.8), channel_id=1, replica_groups=mesh['dp'=32,'param'=16] {'param'}, use_global_device_ids=true, to_apply=%region_15.0 | all-reduce | flops 1 | bytes 8 | tf_op jit(solution)/shard_map/psum | solution.py:44
  950.6 4.6 fusion.14
  955.2 0.0 all-reduce.21.cloned.1.call-update
  955.9 0.9 dynamic-slice_multiply_fusion
  956.8 106.1 %all-reduce.21.cloned.1.call-done = f32[1024,36]{0,1:T(8,128)} async-done(((f32[1024,36]{0,1:T(8,128)}), f32[1024,36]{0,1:T(8,128)}) %all-reduce.21.cloned.1.call-update) | async-done | bytes 147472 | tf_op jit(solution)/shard_map/psum | solution.py:25
  1062.9 1.6 multiply_reduce_fusion.5
  1065.2 0.7 copy.9
  1065.9 75.8 %psum.103 = f32[]{:T(128)} all-reduce(f32[]{:T(128)S(6)} %div.38), channel_id=1, replica_groups=mesh['dp'=32,'param'=16] {'dp'}, use_global_device_ids=true, to_apply=%region_18.0 | all-reduce | flops 1 | bytes 8 | tf_op jit(solution)/shard_map/psum | solution.py:72
  (1 shorter events, 0.0 us)
Async XLA Ops:
  7.2 1.0 copy-start
  7.2 4.5 copy-start.3
  7.2 5.5 copy-start.7
  7.2 117.8 %copy-start.5 = (f32[1024,36]{0,1:T(8,128)S(1)}, f32[1024,36]{0,1:T(8,128)}, u32[]{:S(2)}) copy-start(f32[1024,36]{0,1:T(8,128)} %param.10) | copy-start | bytes 442372
  7.2 117.8 %copy-start.4 = (f32[1024,36]{0,1:T(8,128)S(1)}, f32[1024,36]{0,1:T(8,128)}, u32[]{:S(2)}) copy-start(f32[1024,36]{0,1:T(8,128)} %param.11) | copy-start | bytes 442372
  7.2 117.8 %copy-start.6 = (f32[1024]{0:T(1024)S(1)}, f32[1024]{0:T(1024)}, u32[]{:S(2)}) copy-start(f32[1024]{0:T(1024)} %param.12) | copy-start | bytes 12292
  7.2 117.7 %all-reduce.9.cloned.1.call-start = ((), (), s32[]{:S(2)}) async-start(), calls=%async_computation | async-start | bytes 327680 | tf_op jit(solution)/shard_map/psum | solution.py:25
  12.6 278.6 %all-reduce.11.cloned.1.call-start = ((), (), s32[]{:S(2)}) async-start(), calls=%async_computation.1 | async-start | bytes 2097152 | tf_op jit(solution)/shard_map/psum | solution.py:38
  130.6 270.3 %all-reduce.13.cloned.1.call-start = ((), (), s32[]{:S(2)}) async-start(), calls=%async_computation.2 | async-start | bytes 327680 | tf_op jit(solution)/shard_map/psum | solution.py:25
  295.9 271.1 %copy-start.1 = (f32[2048,128]{0,1:T(8,128)S(1)}, f32[2048,128]{0,1:T(8,128)}, u32[]{:S(2)}) copy-start(f32[2048,128]{0,1:T(8,128)} %all-reduce.11.cloned.1.call-done) | copy-start | bytes 3145732
  295.9 271.1 %all-reduce.15.cloned.1.call-start = ((), (), s32[]{:S(2)}) async-start(), calls=%async_computation.3 | async-start | bytes 2097152 | tf_op jit(solution)/shard_map/psum | solution.py:38
  406.4 325.1 %all-reduce.17.cloned.1.call-start = ((), (), s32[]{:S(2)}) async-start(), calls=%async_computation.4 | async-start | bytes 327680 | tf_op jit(solution)/shard_map/psum | solution.py:25
  567.0 52.4 %copy-start.2 = (f32[2048,128]{0,1:T(8,128)S(1)}, f32[2048,128]{0,1:T(8,128)}, u32[]{:S(2)}) copy-start(f32[2048,128]{0,1:T(8,128)} %all-reduce.15.cloned.1.call-done) | copy-start | bytes 3145732
  623.8 273.8 %all-reduce.19.cloned.1.call-start = ((), (), s32[]{:S(2)}) async-start(), calls=%async_computation.5 | async-start | bytes 2097152 | tf_op jit(solution)/shard_map/psum | solution.py:38
  737.0 325.9 %all-reduce.21.cloned.1.call-start = ((), (), s32[]{:S(2)}) async-start(), calls=%async_computation.6 | async-start | bytes 327680 | tf_op jit(solution)/shard_map/psum | solution.py:25
Sparse Core Ops, SparseCore 0:
  12.7 112.1 all-reduce.8
  130.7 160.5 all-reduce.10
  296.1 104.7 all-reduce.12
  406.5 160.4 all-reduce.14
  623.9 107.4 all-reduce.16
  737.1 160.4 all-reduce.18
  955.3 107.5 all-reduce.20
where the time goes:
time: 1150 us
  waiting for transfers between devices  913 us (79%)
  blocking collectives  167 us (15%)
  matrix products  34.5 us (3%)
  between operations  22.2 us (2%)
  other arithmetic  12.4 us (1%)
    psum x3, waiting for transfers between devices, rowsum(): return lax.psum(term, 'dp')  482 us
    psum x4, waiting for transfers between devices, head_total(): lax.psum(jnp.dot(part, w_head, preferred_element_type=jnp.float32), 'param')  431 us
    psum x4, blocking collectives, total(): return lax.psum((values[0],), 'param')  90.8 us
    psum x1, blocking collectives, shards(): kl_value = lax.psum(jnp.sum(dmean * dmean * inv_var) / (2.0 * batch), 'dp')  75.8 us
  transfers between devices with their start and end apart: 7, of which 7 were waited for; matrix products, arithmetic and copies ran while one was open for 0% of the time, Pallas kernels for 0%

commit v1 on v0

--- a/solution.py
+++ b/solution.py
@@ -35,7 +35,7 @@
         term = lax.dot_general(
             features, grads, (((0,), (0,)), ((), ())), preferred_element_type=jnp.float32
         )
-        return lax.psum(term, "dp")
+        return jnp.sum(lax.all_gather(term, "dp"), axis=0)
 
     def expand(vector_b):
         return jnp.dot(features, vector_b, preferred_element_type=jnp.float32)

time: 1150 us -> 1490 us (1.30)
  waiting for transfers between devices: 913 us -> 1140 us
  local copies, waits for them, and re-layouts: 1.67 us -> 87.3 us
  other arithmetic: 12.4 us -> 29.2 us
    all_gather x0 -> x3, waiting for transfers between devices: none -> 717 us  [rowsum(): return jnp.sum(lax.all_gather(term, 'dp'), axis=0)]
    psum x3 -> x0, waiting for transfers between devices: 482 us -> none  [rowsum(): return lax.psum(term, 'dp')]
    unnamed x17 -> x20, local copies, waits for them, and re-layouts: 1.67 us -> 87.3 us
    reduce_sum x0 -> x3, other arithmetic: none -> 20.5 us  [rowsum(): return jnp.sum(lax.all_gather(term, 'dp'), axis=0)]
where the time goes in v1:
time: 1490 us
  waiting for transfers between devices  1140 us (77%)
  blocking collectives  170 us (11%)
  local copies, waits for them, and re-layouts  87.3 us (6%)
  matrix products  34.2 us (2%)
  other arithmetic  29.2 us (2%)
  between operations  22.2 us (1%)
    all_gather x3, waiting for transfers between devices, rowsum(): return jnp.sum(lax.all_gather(term, 'dp'), axis=0)  717 us
    psum x4, waiting for transfers between devices, head_total(): lax.psum(jnp.dot(part, w_head, preferred_element_type=jnp.float32), 'param')  425 us
    psum x4, blocking collectives, total(): return lax.psum((values[0],), 'param')  94.6 us
    unnamed x20, local copies, waits for them, and re-layouts  87.3 us
    psum x1, blocking collectives, shards(): kl_value = lax.psum(jnp.sum(dmean * dmean * inv_var) / (2.0 * batch), 'dp')  75.8 us
  transfers between devices with their start and end apart: 7, of which 7 were waited for; matrix products, arithmetic and copies ran while one was open for 0% of the time, Pallas kernels for 0%

profile of v1, /device:TPU:8, one launch (start us, length us, event | category | flops | bytes accessed | tf_op | source)
XLA Modules:
  0.0 1486.9 jit_solution(3468643227662195432)
XLA Ops:
  7.2 0.0 copy-start
  7.2 0.0 copy-start.3
  7.2 0.0 copy-start.7
  7.2 0.0 copy-start.5
  7.2 0.0 copy-start.4
  7.2 0.0 copy-start.6
  7.2 0.0 all-reduce.6.cloned.1.call-start
  7.3 0.9 copy-done
  8.2 3.4 fusion.42
  11.7 0.0 copy-done.3
  11.7 0.9 fusion.27
  12.6 0.0 all-reduce.6.cloned.1.call-update
  12.6 0.0 all-gather.7.cloned.1.call-start
  12.7 0.0 copy-done.7
  12.7 112.3 %all-reduce.6.cloned.1.call-done = f32[1024,36]{0,1:T(8,128)} async-done(((f32[1024,36]{0,1:T(8,128)}), f32[1024,36]{0,1:T(8,128)}) %all-reduce.6.cloned.1.call-update) | async-done | bytes 147472 | tf_op jit(solution)/shard_map/psum | solution.py:25
  125.0 0.0 copy-done.5
  125.0 0.0 copy-done.4
  125.0 0.0 copy-done.6
  125.0 1.6 fusion.11
  126.6 3.9 convolution_bitcast_fusion.2
  130.5 0.0 all-gather.7.cloned.1.call-update
  130.6 0.0 all-reduce.8.cloned.1.call-start
  130.6 239.3 %all-gather.7.cloned.1.call-done = f32[65536,128]{0,1:T(8,128)} async-done(((f32[2048,128]{0,1:T(8,128)}), f32[65536,128]{0,1:T(8,128)}) %all-gather.7.cloned.1.call-update) | async-done | bytes 33554448 | tf_op jit(solution)/shard_map/all_gather | solution.py:38
  369.9 28.2 %copy.10 = f32[16,8,32,2048]{3,2,1,0:T(8,128)S(1)} copy(f32[16,8,32,2048]{3,1,2,0:T(8,128)} %bitcast.68) | data formatting | bytes 67108864
  398.1 6.8 bitcast_reduce_fusion.2
  404.9 4.3 fusion.16
  409.2 0.0 all-reduce.8.cloned.1.call-update
  409.2 0.0 all-gather.9.cloned.1.call-start
  409.3 104.2 %all-reduce.8.cloned.1.call-done = f32[1024,36]{0,1:T(8,128)} async-done(((f32[1024,36]{0,1:T(8,128)}), f32[1024,36]{0,1:T(8,128)}) %all-reduce.8.cloned.1.call-update) | async-done | bytes 147472 | tf_op jit(solution)/shard_map/psum | solution.py:25
  513.5 1.6 fusion.10
  515.1 3.9 convolution_bitcast_fusion.1
  519.0 0.0 all-gather.9.cloned.1.call-update
  519.0 0.2 all-reduce.10.cloned.1.call-start
  519.2 239.1 %all-gather.9.cloned.1.call-done = f32[65536,128]{0,1:T(8,128)} async-done(((f32[2048,128]{0,1:T(8,128)}), f32[65536,128]{0,1:T(8,128)}) %all-gather.9.cloned.1.call-update) | async-done | bytes 33554448 | tf_op jit(solution)/shard_map/all_gather | solution.py:38
  758.3 28.2 %copy.11 = f32[16,8,32,2048]{3,2,1,0:T(8,128)S(1)} copy(f32[16,8,32,2048]{3,1,2,0:T(8,128)} %bitcast.69) | data formatting | bytes 67108864
  786.5 6.8 bitcast_reduce_fusion.1
  793.3 0.9 multiply_reduce_fusion.3
  794.3 23.1 %all-reduce = (f32[]{:T(128)}, f32[]{:T(128)}) all-reduce(f32[]{:T(128)} %get-tuple-element.5, f32[]{:T(128)} %get-tuple-element.4), channel_id=1, replica_groups=mesh['dp'=32,'param'=16] {'param'}, use_global_device_ids=true, to_apply=%region_3.0 | all-reduce | flops 2 | bytes 16 | tf_op jit(solution)/shard_map/psum | solution.py:44
  818.7 0.9 multiply_reduce_fusion.2
  819.6 24.2 %psum.74 = f32[]{:T(128)} all-reduce(f32[]{:T(128)} %multiply_reduce_fusion.2), channel_id=1, replica_groups=mesh['dp'=32,'param'=16] {'param'}, use_global_device_ids=true, to_apply=%region_9.0 | all-reduce | flops 1 | bytes 8 | tf_op jit(solution)/shard_map/psum | solution.py:44
  845.1 4.4 fusion.15
  849.5 0.0 all-reduce.10.cloned.1.call-update
  849.5 0.0 all-gather.11.cloned.1.call-start
  849.5 105.4 %all-reduce.10.cloned.1.call-done = f32[1024,36]{0,1:T(8,128)} async-done(((f32[1024,36]{0,1:T(8,128)}), f32[1024,36]{0,1:T(8,128)}) %all-reduce.10.cloned.1.call-update) | async-done | bytes 147472 | tf_op jit(solution)/shard_map/psum | solution.py:25
  954.9 1.6 fusion.9
  956.5 3.9 convolution_bitcast_fusion
  960.4 0.0 all-gather.11.cloned.1.call-update
  960.5 0.3 all-reduce.12.cloned.1.call-start
  960.7 239.0 %all-gather.11.cloned.1.call-done = f32[65536,128]{0,1:T(8,128)} async-done(((f32[2048,128]{0,1:T(8,128)}), f32[65536,128]{0,1:T(8,128)}) %all-gather.11.cloned.1.call-update) | async-done | bytes 33554448 | tf_op jit(solution)/shard_map/all_gather | solution.py:38
  1199.8 28.2 %copy.12 = f32[16,8,32,2048]{3,2,1,0:T(8,128)S(1)} copy(f32[16,8,32,2048]{3,1,2,0:T(8,128)} %bitcast.67) | data formatting | bytes 67108864
  1228.0 6.9 bitcast_reduce_fusion
  1234.9 1.0 copy-done.2
  1235.9 1.0 multiply_reduce_fusion.1
  1236.9 23.1 %psum.76 = f32[]{:T(128)} all-reduce(f32[]{:T(128)} %multiply_reduce_fusion.1), channel_id=1, replica_groups=mesh['dp'=32,'param'=16] {'param'}, use_global_device_ids=true, to_apply=%region_13.0 | all-reduce | flops 1 | bytes 8 | tf_op jit(solution)/shard_map/psum | solution.py:44
  1261.3 0.0 copy-start.1
  1261.3 3.4 multiply_reduce_fusion
  1264.8 24.2 %psum.77 = f32[]{:T(128)} all-reduce(f32[]{:T(128)} %get-tuple-element.8), channel_id=1, replica_groups=mesh['dp'=32,'param'=16] {'param'}, use_global_device_ids=true, to_apply=%region_15.0 | all-reduce | flops 1 | bytes 8 | tf_op jit(solution)/shard_map/psum | solution.py:44
  1289.6 4.6 fusion.14
  1294.2 0.0 all-reduce.12.cloned.1.call-update
  1295.0 0.9 dynamic-slice_multiply_fusion
  1295.9 103.6 %all-reduce.12.cloned.1.call-done = f32[1024,36]{0,1:T(8,128)} async-done(((f32[1024,36]{0,1:T(8,128)}), f32[1024,36]{0,1:T(8,128)}) %all-reduce.12.cloned.1.call-update) | async-done | bytes 147472 | tf_op jit(solution)/shard_map/psum | solution.py:25
  1399.5 1.6 multiply_reduce_fusion.5
  1401.8 0.7 copy.9
  1402.5 75.8 %psum.79 = f32[]{:T(128)} all-reduce(f32[]{:T(128)S(6)} %div.38), channel_id=1, replica_groups=mesh['dp'=32,'param'=16] {'dp'}, use_global_device_ids=true, to_apply=%region_18.0 | all-reduce | flops 1 | bytes 8 | tf_op jit(solution)/shard_map/psum | solution.py:72
  (3 shorter events, 0.0 us)
Async XLA Ops:
  7.2 1.1 copy-start
  7.2 4.5 copy-start.3
  7.2 5.5 copy-start.7
  7.2 117.8 %copy-start.5 = (f32[1024,36]{0,1:T(8,128)S(1)}, f32[1024,36]{0,1:T(8,128)}, u32[]{:S(2)}) copy-start(f32[1024,36]{0,1:T(8,128)} %param.10) | copy-start | bytes 442372
  7.2 117.8 %copy-start.4 = (f32[1024,36]{0,1:T(8,128)S(1)}, f32[1024,36]{0,1:T(8,128)}, u32[]{:S(2)}) copy-start(f32[1024,36]{0,1:T(8,128)} %param.11) | copy-start | bytes 442372
  7.2 117.8 %copy-start.6 = (f32[1024]{0:T(1024)S(1)}, f32[1024]{0:T(1024)}, u32[]{:S(2)}) copy-start(f32[1024]{0:T(1024)} %param.12) | copy-start | bytes 12292
  7.2 117.8 %all-reduce.6.cloned.1.call-start = ((), (), s32[]{:S(2)}) async-start(), calls=%async_computation | async-start | bytes 327680 | tf_op jit(solution)/shard_map/psum | solution.py:25
  12.6 357.2 %all-gather.7.cloned.1.call-start = ((), (), s32[]{:S(2)}) async-start(), calls=%async_computation.4 | async-start | bytes 34603008 | tf_op jit(solution)/shard_map/all_gather | solution.py:38
  130.6 382.9 %all-reduce.8.cloned.1.call-start = ((), (), s32[]{:S(2)}) async-start(), calls=%async_computation.1 | async-start | bytes 327680 | tf_op jit(solution)/shard_map/psum | solution.py:25
  409.2 349.1 %all-gather.9.cloned.1.call-start = ((), (), s32[]{:S(2)}) async-start(), calls=%async_computation.5 | async-start | bytes 34603008 | tf_op jit(solution)/shard_map/all_gather | solution.py:38
  519.0 435.9 %all-reduce.10.cloned.1.call-start = ((), (), s32[]{:S(2)}) async-start(), calls=%async_computation.2 | async-start | bytes 327680 | tf_op jit(solution)/shard_map/psum | solution.py:25
  849.5 350.3 %all-gather.11.cloned.1.call-start = ((), (), s32[]{:S(2)}) async-start(), calls=%async_computation.6 | async-start | bytes 34603008 | tf_op jit(solution)/shard_map/all_gather | solution.py:38
  960.5 439.0 %all-reduce.12.cloned.1.call-start = ((), (), s32[]{:S(2)}) async-start(), calls=%async_computation.3 | async-start | bytes 327680 | tf_op jit(solution)/shard_map/psum | solution.py:25
  1234.9 1.0 copy-start.2
  1261.3 217.6 %copy-start.1 = (bf16[2048,128]{1,0:T(8,128)(2,1)S(1)}, bf16[2048,128]{1,0:T(8,128)(2,1)}, u32[]{:S(2)}) copy-start(bf16[2048,128]{1,0:T(8,128)(2,1)} %param.8) | copy-start | bytes 1572868
Sparse Core Ops, SparseCore 0:
  12.7 112.2 all-reduce.5
  130.7 239.1 all-gather.6
  409.4 104.0 all-reduce.7
  519.1 239.1 all-gather.8
  849.6 105.2 all-reduce.9
  960.6 239.1 all-gather.10
  1294.4 105.1 all-reduce.11
